TPU v7x, 32 devices: a whole 2x2x4 slice. The times are simulated.
32 devices in a mesh: dp: 8 (over y, x, core), fsdp: 4 (over z).
Axes of the slice: x: 2, y: 2, z: 4, core: 2. Of those that a mesh axis runs over, the one named last changes fastest.
Arguments:
- gene_ids: int32 [32, 2048], P(('dp', 'fsdp')), may hold values from 0 to 12799
- expr_bins: int32 [32, 2048], P(('dp', 'fsdp')), may hold values from 0 to 63
- study_ids: int32 [32], P(('dp', 'fsdp')), may hold values from 0 to 63
- lengths: int32 [32], P(('dp', 'fsdp')), may hold values from 256 to 2048, as said below
- prior_embed: bfloat16 [32, 2048, 256], P(('dp', 'fsdp')), may hold values from -3 to 3
- cotangent: bfloat16 [32, 2048, 256], P(('dp', 'fsdp')), may hold values from -6 to 6
- gene_table: bfloat16 [12800, 256], P('fsdp'), may hold values from -3 to 3
- expr_table: bfloat16 [64, 256], P('fsdp'), may hold values from -3 to 3
- study_table: bfloat16 [64, 256], P('fsdp'), may hold values from -3 to 3
- position_table: bfloat16 [2048, 256], P('fsdp'), may hold values from -3 to 3
- norm1_gain: bfloat16 [256], P('fsdp'), may hold values from 0.099609375 to 1.8984375
- norm1_shift: bfloat16 [256], P('fsdp'), may hold values from -1.5 to 1.5
- w_qkv: bfloat16 [256, 768], P('fsdp'), may hold values from -0.375 to 0.375
- bias_query: bfloat16 [256], P('fsdp'), may hold values from -1.5 to 1.5
- bias_value: bfloat16 [256], P('fsdp'), may hold values from -1.5 to 1.5
- w_output: bfloat16 [256, 256], P('fsdp'), may hold values from -6 to 6
- bias_output: bfloat16 [256], P('fsdp'), may hold values from -1.5 to 1.5
- norm2_gain: bfloat16 [256], P('fsdp'), may hold values from 0.099609375 to 1.8984375
- norm2_shift: bfloat16 [256], P('fsdp'), may hold values from -1.5 to 1.5
- w_up_proj: bfloat16 [256, 512], P('fsdp'), may hold values from -0.375 to 0.375
- bias_up: bfloat16 [512], P('fsdp'), may hold values from -1.5 to 1.5
- w_down_proj: bfloat16 [512, 256], P('fsdp'), may hold values from -0.25 to 0.25
- bias_down: bfloat16 [256], P('fsdp'), may hold values from -1.5 to 1.5
Outputs:
- hidden_out: bfloat16 [32, 2048, 256], P(('dp', 'fsdp'))
- grad_gene_table: float32 [12800, 256], P('fsdp')
- update_count: int32 [12800], P('fsdp')
- grad_expr_table: float32 [64, 256], P('fsdp')
- grad_study_table: float32 [64, 256], P('fsdp')
- grad_position_table: float32 [2048, 256], P('fsdp')
- grad_norm1_gain: float32 [256], P('fsdp')
- grad_norm1_shift: float32 [256], P('fsdp')
- grad_w_qkv: float32 [256, 768], P('fsdp')
- grad_bias_query: float32 [256], P('fsdp')
- grad_bias_value: float32 [256], P('fsdp')
- grad_w_output: float32 [256, 256], P('fsdp')
- grad_bias_output: float32 [256], P('fsdp')
- grad_norm2_gain: float32 [256], P('fsdp')
- grad_norm2_shift: float32 [256], P('fsdp')
- grad_w_up_proj: float32 [256, 512], P('fsdp')
- grad_bias_up: float32 [512], P('fsdp')
- grad_w_down_proj: float32 [512, 256], P('fsdp')
- grad_bias_down: float32 [256], P('fsdp')
Inputs may be any that keep to these rules, and one draw needn't show every extreme that they name: Slots from lengths[c] on are padding; some cell has 2048 genes and some 2048 // 8.
All inputs are finite; a program needn't handle non-finite values.
Results may differ from a plain program's by a relative error of at most 0.0082.
Values may be sent and summed in bfloat16 or wider, within the bound.
No kernel may reach another device: no remote copies, remote signals or barrier semaphores. Data moves between devices by JAX's collectives and lax.ppermute only.
A program may use at most 128 MiB of HBM per device.

v0:
```python
import jax
import jax.numpy as jnp
from jax import lax
from jax.sharding import PartitionSpec as P

HEADS = 4
epsilon = 1e-05
highest = lax.Precision.HIGHEST


def normalize(values):
    average = jnp.mean(values, axis=-1, keepdims=True)
    centered = values - average
    variance = jnp.mean(centered * centered, axis=-1, keepdims=True)
    return centered * lax.rsqrt(variance + epsilon)


def norm_back(values, gain, grad):
    unused, pullback = jax.vjp(lambda entries, scale: normalize(entries) * scale, values, gain)
    grad_rows, grad_gain = pullback(grad)
    return (grad_rows, grad_gain, jnp.sum(grad, axis=0))


def matmul(left, right):
    return jnp.dot(left, right, preferred_element_type=jnp.float32)


def weight_grad(left, right):
    return lax.dot_general(
        left, right, (((0,), (0,)), ((), ())), preferred_element_type=jnp.float32
    )


def back_matmul(left, right):
    return lax.dot_general(
        left, right, (((1,), (1,)), ((), ())), preferred_element_type=jnp.float32
    )


def table_grad(hits, grads):
    return lax.dot_general(
        hits, grads, (((0,), (0,)), ((), ())), precision=highest, preferred_element_type=jnp.float32
    )


def attend(query, keys, values, key_mask, block):
    length, heads, head_size = query.shape
    scale = head_size ** (-0.5)
    query_blocks = query.reshape(length // block, block, heads, head_size)

    def one_block(query_block):
        scores = (
            jnp.einsum("qhk,shk->hqs", query_block, keys, preferred_element_type=jnp.float32)
            * scale
        )
        scores = jnp.where(key_mask[None, None, :] > 0, scores, -1000000000.0)
        peak = jnp.max(scores, axis=-1, keepdims=True)
        raised = jnp.exp(scores - peak)
        total = jnp.sum(raised, axis=-1, keepdims=True)
        probs = (raised / total).astype(jnp.bfloat16)
        attended = jnp.einsum("hqs,shk->qhk", probs, values, preferred_element_type=jnp.float32)
        return (attended.astype(jnp.bfloat16), (peak + jnp.log(total))[..., 0])

    attended, log_total = lax.map(one_block, query_blocks)
    return (attended.reshape(length, heads, head_size), log_total)


def attend_back(query, keys, values, key_mask, log_total, grad_attended, block):
    length, heads, head_size = query.shape
    scale = head_size ** (-0.5)
    query_blocks = query.reshape(length // block, block, heads, head_size)
    grad_blocks = grad_attended.reshape(length // block, block, heads, head_size)

    def one_block(carry, embedding_parts):
        grad_keys, grad_values = carry
        query_block, grad_block, log_block = embedding_parts
        scores = (
            jnp.einsum("qhk,shk->hqs", query_block, keys, preferred_element_type=jnp.float32)
            * scale
        )
        scores = jnp.where(key_mask[None, None, :] > 0, scores, -1000000000.0)
        probs = jnp.exp(scores - log_block[..., None])
        probs_low = probs.astype(jnp.bfloat16)
        grad_probs = jnp.einsum(
            "qhk,shk->hqs", grad_block, values, preferred_element_type=jnp.float32
        )
        inner = jnp.sum(probs * grad_probs, axis=-1, keepdims=True)
        grad_scores = (probs * (grad_probs - inner)).astype(jnp.bfloat16)
        grad_query = (
            jnp.einsum("hqs,shk->qhk", grad_scores, keys, preferred_element_type=jnp.float32)
            * scale
        )
        grad_keys = (
            grad_keys
            + jnp.einsum(
                "hqs,qhk->shk", grad_scores, query_block, preferred_element_type=jnp.float32
            )
            * scale
        )
        grad_values = grad_values + jnp.einsum(
            "hqs,qhk->shk", probs_low, grad_block, preferred_element_type=jnp.float32
        )
        return ((grad_keys, grad_values), grad_query)

    starting = jnp.zeros((length, heads, head_size), jnp.float32)
    (grad_keys, grad_values), grad_query = lax.scan(
        one_block, (starting, starting), (query_blocks, grad_blocks, log_total)
    )
    return (grad_query.reshape(length, heads, head_size), grad_keys, grad_values)


def body(
    gene_ids,
    expr_bins,
    study_ids,
    lengths,
    prior_embed,
    cotangent,
    gene_table,
    expr_table,
    study_table,
    position_table,
    norm1_gain,
    norm1_shift,
    w_qkv,
    bias_query,
    bias_value,
    w_output,
    bias_output,
    norm2_gain,
    norm2_shift,
    w_up_proj,
    bias_up,
    w_down_proj,
    bias_down,
):
    (
        full_gene,
        full_expr,
        full_study,
        full_position,
        gain_one,
        shift_one,
        full_qkv,
        query_bias,
        value_bias,
        full_output,
        output_bias,
        gain_two,
        shift_two,
        full_up,
        up_bias,
        full_down,
        down_bias,
    ) = (
        lax.all_gather(gene_table, "fsdp", axis=0, tiled=True),
        lax.all_gather(expr_table, "fsdp", axis=0, tiled=True),
        lax.all_gather(study_table, "fsdp", axis=0, tiled=True),
        lax.all_gather(position_table, "fsdp", axis=0, tiled=True),
        lax.all_gather(norm1_gain, "fsdp", axis=0, tiled=True),
        lax.all_gather(norm1_shift, "fsdp", axis=0, tiled=True),
        lax.all_gather(w_qkv, "fsdp", axis=0, tiled=True),
        lax.all_gather(bias_query, "fsdp", axis=0, tiled=True),
        lax.all_gather(bias_value, "fsdp", axis=0, tiled=True),
        lax.all_gather(w_output, "fsdp", axis=0, tiled=True),
        lax.all_gather(bias_output, "fsdp", axis=0, tiled=True),
        lax.all_gather(norm2_gain, "fsdp", axis=0, tiled=True),
        lax.all_gather(norm2_shift, "fsdp", axis=0, tiled=True),
        lax.all_gather(w_up_proj, "fsdp", axis=0, tiled=True),
        lax.all_gather(bias_up, "fsdp", axis=0, tiled=True),
        lax.all_gather(w_down_proj, "fsdp", axis=0, tiled=True),
        lax.all_gather(bias_down, "fsdp", axis=0, tiled=True),
    )
    cells, length = gene_ids.shape
    width = full_gene.shape[1]
    rows = cells * length
    heads = HEADS
    head_size = width // heads
    block = min(512, length)

    def shaped(array):
        return array.reshape(cells, length, heads, head_size)

    key_mask = (lax.broadcasted_iota(jnp.int32, (cells, length), 1) < lengths[:, None]).astype(
        jnp.float32
    )
    flat_mask = key_mask.reshape(rows, 1)
    embedded = (
        full_gene[gene_ids].astype(jnp.float32)
        + full_expr[expr_bins].astype(jnp.float32)
        + full_study[study_ids].astype(jnp.float32)[:, None, :]
        + full_position.astype(jnp.float32)[None]
        + prior_embed.astype(jnp.float32)
    )
    inputs = (embedded * key_mask[..., None]).reshape(rows, width)
    normed_one = (
        normalize(inputs) * gain_one.astype(jnp.float32) + shift_one.astype(jnp.float32)
    ).astype(jnp.bfloat16)
    mixed = matmul(normed_one, full_qkv)
    query = (mixed[:, :width] + query_bias.astype(jnp.float32)).astype(jnp.bfloat16)
    keys = mixed[:, width : 2 * width].astype(jnp.bfloat16)
    values = (mixed[:, 2 * width :] + value_bias.astype(jnp.float32)).astype(jnp.bfloat16)
    attended, log_total = lax.map(
        lambda embedding_parts: attend(
            embedding_parts[0], embedding_parts[1], embedding_parts[2], embedding_parts[3], block
        ),
        (shaped(query), shaped(keys), shaped(values), key_mask),
    )
    attended = attended.reshape(rows, width)
    branch = matmul(attended, full_output) + output_bias.astype(jnp.float32)
    middle = inputs + branch
    normed_two = (
        normalize(middle) * gain_two.astype(jnp.float32) + shift_two.astype(jnp.float32)
    ).astype(jnp.bfloat16)
    upward = matmul(normed_two, full_up) + up_bias.astype(jnp.float32)
    activated = jax.nn.gelu(upward, approximate=False).astype(jnp.bfloat16)
    result = (middle + (matmul(activated, full_down) + down_bias.astype(jnp.float32))) * flat_mask
    hidden_out = result.astype(jnp.bfloat16).reshape(cells, length, width)
    back_gain_one, back_qkv, back_output, back_gain_two, back_up, back_down = (
        lax.all_gather(norm1_gain, "fsdp", axis=0, tiled=True),
        lax.all_gather(w_qkv, "fsdp", axis=0, tiled=True),
        lax.all_gather(w_output, "fsdp", axis=0, tiled=True),
        lax.all_gather(norm2_gain, "fsdp", axis=0, tiled=True),
        lax.all_gather(w_up_proj, "fsdp", axis=0, tiled=True),
        lax.all_gather(w_down_proj, "fsdp", axis=0, tiled=True),
    )
    grad_result = cotangent.astype(jnp.float32).reshape(rows, width) * flat_mask
    grad_low = grad_result.astype(jnp.bfloat16)
    grad_down_w = weight_grad(activated, grad_low)
    grad_down_b = jnp.sum(grad_result, axis=0)
    grad_activated = back_matmul(grad_low, back_down)
    unused, gelu_pull = jax.vjp(lambda entries: jax.nn.gelu(entries, approximate=False), upward)
    grad_upward = gelu_pull(grad_activated)[0].astype(jnp.bfloat16)
    grad_up_w = weight_grad(normed_two, grad_upward)
    grad_up_b = jnp.sum(grad_upward.astype(jnp.float32), axis=0)
    grad_normed_two = back_matmul(grad_upward, back_up)
    grad_mid_norm, grad_gain_two, grad_shift_two = norm_back(
        middle, back_gain_two.astype(jnp.float32), grad_normed_two
    )
    grad_middle = grad_result + grad_mid_norm
    grad_branch = grad_middle.astype(jnp.bfloat16)
    grad_output_w = weight_grad(attended, grad_branch)
    grad_output_b = jnp.sum(grad_branch.astype(jnp.float32), axis=0)
    grad_attended = back_matmul(grad_branch, back_output).astype(jnp.bfloat16)
    grad_query, grad_keys, grad_values = lax.map(
        lambda embedding_parts: attend_back(
            embedding_parts[0],
            embedding_parts[1],
            embedding_parts[2],
            embedding_parts[3],
            embedding_parts[4],
            embedding_parts[5],
            block,
        ),
        (shaped(query), shaped(keys), shaped(values), key_mask, log_total, shaped(grad_attended)),
    )
    grad_query = grad_query.reshape(rows, width).astype(jnp.bfloat16)
    grad_keys = grad_keys.reshape(rows, width).astype(jnp.bfloat16)
    grad_values = grad_values.reshape(rows, width).astype(jnp.bfloat16)
    grad_mixed = jnp.concatenate([grad_query, grad_keys, grad_values], axis=1)
    grad_qkv_w = weight_grad(normed_one, grad_mixed)
    grad_query_b = jnp.sum(grad_query.astype(jnp.float32), axis=0)
    grad_value_b = jnp.sum(grad_values.astype(jnp.float32), axis=0)
    grad_normed_one = back_matmul(grad_mixed, back_qkv)
    grad_in_norm, grad_gain_one, grad_shift_one = norm_back(
        inputs, back_gain_one.astype(jnp.float32), grad_normed_one
    )
    grad_inputs = (grad_middle + grad_in_norm) * flat_mask
    grad_cells = grad_inputs.reshape(cells, length, width)
    bin_hits = (
        expr_bins.reshape(rows, 1) == lax.broadcasted_iota(jnp.int32, (1, full_expr.shape[0]), 1)
    ).astype(jnp.float32)
    grad_expr = table_grad(bin_hits, grad_inputs)
    study_hits = (
        study_ids[:, None] == lax.broadcasted_iota(jnp.int32, (1, full_study.shape[0]), 1)
    ).astype(jnp.float32)
    grad_study = table_grad(study_hits, jnp.sum(grad_cells, axis=1))
    grad_position = jnp.sum(grad_cells, axis=0)
    flat_ids = gene_ids.reshape(rows)
    vocab = full_gene.shape[0]
    dense_grad = jnp.zeros((vocab, width), jnp.float32).at[flat_ids].add(grad_inputs)
    dense_count = jnp.zeros((vocab,), jnp.float32).at[flat_ids].add(flat_mask[:, 0])
    (
        table_share,
        count_share,
        expr_share,
        study_share,
        position_share,
        gain_one_share,
        shift_one_share,
        qkv_share,
        query_b_share,
        value_b_share,
        output_share,
        output_b_share,
        gain_two_share,
        shift_two_share,
        up_share,
        up_b_share,
        down_share,
        down_b_share,
    ) = (
        lax.psum_scatter(dense_grad, "fsdp", scatter_dimension=0, tiled=True),
        lax.psum_scatter(dense_count, "fsdp", scatter_dimension=0, tiled=True),
        lax.psum_scatter(grad_expr, "fsdp", scatter_dimension=0, tiled=True),
        lax.psum_scatter(grad_study, "fsdp", scatter_dimension=0, tiled=True),
        lax.psum_scatter(grad_position, "fsdp", scatter_dimension=0, tiled=True),
        lax.psum_scatter(grad_gain_one, "fsdp", scatter_dimension=0, tiled=True),
        lax.psum_scatter(grad_shift_one, "fsdp", scatter_dimension=0, tiled=True),
        lax.psum_scatter(grad_qkv_w, "fsdp", scatter_dimension=0, tiled=True),
        lax.psum_scatter(grad_query_b, "fsdp", scatter_dimension=0, tiled=True),
        lax.psum_scatter(grad_value_b, "fsdp", scatter_dimension=0, tiled=True),
        lax.psum_scatter(grad_output_w, "fsdp", scatter_dimension=0, tiled=True),
        lax.psum_scatter(grad_output_b, "fsdp", scatter_dimension=0, tiled=True),
        lax.psum_scatter(grad_gain_two, "fsdp", scatter_dimension=0, tiled=True),
        lax.psum_scatter(grad_shift_two, "fsdp", scatter_dimension=0, tiled=True),
        lax.psum_scatter(grad_up_w, "fsdp", scatter_dimension=0, tiled=True),
        lax.psum_scatter(grad_up_b, "fsdp", scatter_dimension=0, tiled=True),
        lax.psum_scatter(grad_down_w, "fsdp", scatter_dimension=0, tiled=True),
        lax.psum_scatter(grad_down_b, "fsdp", scatter_dimension=0, tiled=True),
    )
    (
        table_sum,
        count_sum,
        expr_sum,
        study_sum,
        position_sum,
        gain_one_sum,
        shift_one_sum,
        qkv_sum,
        query_b_sum,
        value_b_sum,
        output_sum,
        output_b_sum,
        gain_two_sum,
        shift_two_sum,
        up_sum,
        up_b_sum,
        down_sum,
        down_b_sum,
    ) = lax.psum(
        (
            table_share,
            count_share,
            expr_share,
            study_share,
            position_share,
            gain_one_share,
            shift_one_share,
            qkv_share,
            query_b_share,
            value_b_share,
            output_share,
            output_b_share,
            gain_two_share,
            shift_two_share,
            up_share,
            up_b_share,
            down_share,
            down_b_share,
        ),
        "dp",
    )
    return (
        hidden_out,
        table_sum,
        count_sum.astype(jnp.int32),
        expr_sum,
        study_sum,
        position_sum,
        gain_one_sum,
        shift_one_sum,
        qkv_sum,
        query_b_sum,
        value_b_sum,
        output_sum,
        output_b_sum,
        gain_two_sum,
        shift_two_sum,
        up_sum,
        up_b_sum,
        down_sum,
        down_b_sum,
    )


def solution(mesh):
    return jax.shard_map(
        body,
        mesh=mesh,
        in_specs=(
            P(("dp", "fsdp"), None),
            P(("dp", "fsdp"), None),
            P(("dp", "fsdp")),
            P(("dp", "fsdp")),
            P(("dp", "fsdp"), None, None),
            P(("dp", "fsdp"), None, None),
            P("fsdp", None),
            P("fsdp", None),
            P("fsdp", None),
            P("fsdp", None),
            P("fsdp"),
            P("fsdp"),
            P("fsdp", None),
            P("fsdp"),
            P("fsdp"),
            P("fsdp", None),
            P("fsdp"),
            P("fsdp"),
            P("fsdp"),
            P("fsdp", None),
            P("fsdp"),
            P("fsdp", None),
            P("fsdp"),
        ),
        out_specs=(
            P(("dp", "fsdp"), None, None),
            P("fsdp", None),
            P("fsdp"),
            P("fsdp", None),
            P("fsdp", None),
            P("fsdp", None),
            P("fsdp"),
            P("fsdp"),
            P("fsdp", None),
            P("fsdp"),
            P("fsdp"),
            P("fsdp", None),
            P("fsdp"),
            P("fsdp"),
            P("fsdp"),
            P("fsdp", None),
            P("fsdp"),
            P("fsdp", None),
            P("fsdp"),
        ),
        check_vma=False,
    )
```

profile of v0, /device:TPU:0, one launch (start us, length us, event | category | flops | bytes accessed | tf_op | source)
XLA Modules:
  0.0 905.6 jit_solution(10123542352486221909)
XLA Ops:
  20.7 16.2 %all-reduce.21 = (bf16[256]{0:T(256)(128)(2,1)S(1)}, bf16[256]{0:T(256)(128)(2,1)S(1)}, bf16[256]{0:T(256)(128)(2,1)S(1)}, bf16[256]{0:T(256)(128)(2,1)S(1)}, bf...) all-reduce(bf16[256]{0:T(256)(128)(2,1)S(1)} %dynamic-update-slice., ...), channel_id=1, replica_groups=mesh['dp'=8,'fsdp'=4] {'fsdp'}, use_global_device_ids=true, to_apply=%add.1 | all-reduce | flops 2048 | bytes 8192
  49.2 16.0 %all_gather.58 = bf16[64,256]{1,0:T(8,128)(2,1)S(1)} all-gather(bf16[16,256]{1,0:T(8,128)(2,1)} %param.34), channel_id=1, replica_groups=mesh['dp'=8,'fsdp'=4] {'fsdp'}, dimensions={0}, use_global_device_ids=true | all-gather | bytes 40960 | tf_op jit(solution)/shard_map/all_gather | solution.py:157
  76.3 15.8 %all_gather.59 = bf16[64,256]{1,0:T(8,128)(2,1)S(1)} all-gather(bf16[16,256]{1,0:T(8,128)(2,1)S(1)} %copy-done.55), channel_id=1, replica_groups=mesh['dp'=8,'fsdp'=4] {'fsdp'}, dimensions={0}, use_global_device_ids=true | all-gather | bytes 40960 | tf_op jit(solution)/shard_map/all_gather | solution.py:158
  92.2 18.9 %all_gather.66 = bf16[256,256]{1,0:T(8,128)(2,1)} all-gather(bf16[64,256]{1,0:T(8,128)(2,1)S(1)} %copy-done.49), channel_id=1, replica_groups=mesh['dp'=8,'fsdp'=4] {'fsdp'}, dimensions={0}, use_global_device_ids=true | all-gather | bytes 163840 | tf_op jit(solution)/shard_map/all_gather | solution.py:165
  111.1 22.1 %all_gather.70 = bf16[256,512]{1,0:T(8,128)(2,1)} all-gather(bf16[64,512]{1,0:T(8,128)(2,1)S(1)} %copy-done.44), channel_id=1, replica_groups=mesh['dp'=8,'fsdp'=4] {'fsdp'}, dimensions={0}, use_global_device_ids=true | all-gather | bytes 327680 | tf_op jit(solution)/shard_map/all_gather | solution.py:169
  133.2 16.9 %all_gather.72 = bf16[512,256]{1,0:T(8,128)(2,1)} all-gather(bf16[128,256]{1,0:T(8,128)(2,1)S(1)} %copy-done.45), channel_id=1, replica_groups=mesh['dp'=8,'fsdp'=4] {'fsdp'}, dimensions={0}, use_global_device_ids=true | all-gather | bytes 327680 | tf_op jit(solution)/shard_map/all_gather | solution.py:171
  150.7 17.1 %all_gather.63 = bf16[256,768]{1,0:T(8,128)(2,1)S(1)} all-gather(bf16[64,768]{1,0:T(8,128)(2,1)} %param.39), channel_id=1, replica_groups=mesh['dp'=8,'fsdp'=4] {'fsdp'}, dimensions={0}, use_global_device_ids=true | all-gather | bytes 491520 | tf_op jit(solution)/shard_map/all_gather | solution.py:162
  167.8 12.3 %gather_fusion = bf16[2048,256]{1,0:T(8,128)(2,1)} fusion(bf16[12800,256]{1,0:T(8,128)(2,1)} %all-gather.4.cloned.1.call-done, s32[2048]{0:T(1024)S(1)} %broadcast_clamp_fusion.1), kind=kCustom, calls=%fused_computation | custom fusion | bytes 2105344 | tf_op jit(solution)/shard_map/gather | solution.py:189
  191.9 53.9 %while.49 = (s32[]{:T(128)}, bf16[4,512,4,64]{1,3,2,0:T(8,128)(2,1)}, f32[4,4,512]{2,1,0:T(4,128)S(1)}, bf16[4,512,4,64]{1,3,2,0:T(8,128)(2,1)}, bf16[2048,4,64]...) while((s32[]{:T(128)}, bf16[4,512,4,64]{1,3,2,0:T(8,128)(2,1)}, ...), condition=%wide.region_5.6_spmd.clone, body=%wide.region_2.5_spmd.clone.sunk | while | flops 1124208640 | bytes 53026924 | solution.py:64
  249.5 10.9 %multiply_convert_fusion.1 = (bf16[2048,512]{1,0:T(8,128)(2,1)}, f32[2048,512]{1,0:T(8,128)S(1)}, f32[2048,512]{1,0:T(8,128)S(1)}) fusion(f32[512]{0:T(512)S(1)} %bitcast.190, bf16[256,512]{1,0:T(8,128)(2,1)S(1)} %copy-done.26, f32[2048,256]{0,1:T(8,128)S(1)} %get-tuple-element.435, f32[256]{0:T(256)S(1)} %copy-done.72, f32[256]{0:T(256)S(1)} %copy-done.64, ...), kind=kOutput, calls=%fused_computation.63 | convolution fusion | flops 608698368 | bytes 12865536 | tf_op jit(solution)/shard_map/dot_general | solution.py:25
  297.0 166.8 %while.50 = (s32[]{:T(128)}, f32[2048,4,64]{0,2,1:T(8,128)}, f32[2048,4,64]{0,2,1:T(8,128)}, bf16[4,512,4,64]{1,3,2,0:T(8,128)(2,1)}, bf16[4,512,4,64]{1,3,2,0:T...) while((s32[]{:T(128)}, f32[2048,4,64]{0,2,1:T(8,128)}, ...), condition=%wide.region_12.13_spmd.clone, body=%wide.region_10.12_spmd.clone.sunk | while | flops 2750025728 | bytes 172556464 | solution.py:106
  306.8 9.5 %multiply_reduce_fusion.8 = (f32[4,512]{1,0:T(4,128)S(1)}, f32[4,512,2048]{2,1,0:T(8,128)}) fusion(f32[4,512,2048]{2,1,0:T(8,128)S(1)} %fusion.154, f32[4,512]{1,0:T(4,128)S(1)} %dynamic-slice_bitcast_fusion.2, pred[2048]{0:T(1024)(128)(4,1)S(1)} %convert_compare_fusion.5, bf16[2048,4,64]{0,2,1:T(8,128)(2,1)S(1)} %get-tuple-element.611, ...), kind=kOutput, calls=%fused_computation.25.clone.1 | convolution fusion | flops 557840384 | bytes 34883588 | tf_op jit(solution)/shard_map/while/body/eval_jaxpr/while/body/eval_jaxpr/qhk,shk->hqs/dot_general | solution.py:84
  316.4 10.8 %multiply_convert_fusion.3 = bf16[4,512,2048]{2,1,0:T(8,128)(2,1)} fusion(f32[4,512,2048]{2,1,0:T(8,128)} %get-tuple-element.553, f32[4,512,2048]{2,1,0:T(8,128)S(1)} %fusion.154, f32[4,512]{1,0:T(4,128)S(1)} %get-tuple-element.554, f32[4,512]{1,0:T(4,128)S(1)} %dynamic-slice_bitcast_fusion.2, pred[2048]{0:T(1024)(128)(4,1)S(1)} %convert_compare_fusion.5), kind=kLoop, calls=%fused_computation.24.clone.1 | loop fusion | flops 25165824 | bytes 41961472 | tf_op jit(solution)/shard_map/while/body/eval_jaxpr/while/body/eval_jaxpr/convert_element_type | solution.py:88
  357.7 10.7 %multiply_convert_fusion.3 = bf16[4,512,2048]{2,1,0:T(8,128)(2,1)} fusion(f32[4,512,2048]{2,1,0:T(8,128)} %get-tuple-element.553, f32[4,512,2048]{2,1,0:T(8,128)S(1)} %fusion.154, f32[4,512]{1,0:T(4,128)S(1)} %get-tuple-element.554, f32[4,512]{1,0:T(4,128)S(1)} %dynamic-slice_bitcast_fusion.2, pred[2048]{0:T(1024)(128)(4,1)S(1)} %convert_compare_fusion.5), kind=kLoop, calls=%fused_computation.24.clone.1 | loop fusion | flops 25165824 | bytes 41961472 | tf_op jit(solution)/shard_map/while/body/eval_jaxpr/while/body/eval_jaxpr/convert_element_type | solution.py:88
  390.0 9.5 %multiply_reduce_fusion.8 = (f32[4,512]{1,0:T(4,128)S(1)}, f32[4,512,2048]{2,1,0:T(8,128)}) fusion(f32[4,512,2048]{2,1,0:T(8,128)S(1)} %fusion.154, f32[4,512]{1,0:T(4,128)S(1)} %dynamic-slice_bitcast_fusion.2, pred[2048]{0:T(1024)(128)(4,1)S(1)} %convert_compare_fusion.5, bf16[2048,4,64]{0,2,1:T(8,128)(2,1)S(1)} %get-tuple-element.611, ...), kind=kOutput, calls=%fused_computation.25.clone.1 | convolution fusion | flops 557840384 | bytes 34883588 | tf_op jit(solution)/shard_map/while/body/eval_jaxpr/while/body/eval_jaxpr/qhk,shk->hqs/dot_general | solution.py:84
  399.5 10.7 %multiply_convert_fusion.3 = bf16[4,512,2048]{2,1,0:T(8,128)(2,1)} fusion(f32[4,512,2048]{2,1,0:T(8,128)} %get-tuple-element.553, f32[4,512,2048]{2,1,0:T(8,128)S(1)} %fusion.154, f32[4,512]{1,0:T(4,128)S(1)} %get-tuple-element.554, f32[4,512]{1,0:T(4,128)S(1)} %dynamic-slice_bitcast_fusion.2, pred[2048]{0:T(1024)(128)(4,1)S(1)} %convert_compare_fusion.5), kind=kLoop, calls=%fused_computation.24.clone.1 | loop fusion | flops 25165824 | bytes 41961472 | tf_op jit(solution)/shard_map/while/body/eval_jaxpr/while/body/eval_jaxpr/convert_element_type | solution.py:88
  441.4 10.7 %multiply_convert_fusion.3 = bf16[4,512,2048]{2,1,0:T(8,128)(2,1)} fusion(f32[4,512,2048]{2,1,0:T(8,128)} %get-tuple-element.553, f32[4,512,2048]{2,1,0:T(8,128)S(1)} %fusion.154, f32[4,512]{1,0:T(4,128)S(1)} %get-tuple-element.554, f32[4,512]{1,0:T(4,128)S(1)} %dynamic-slice_bitcast_fusion.2, pred[2048]{0:T(1024)(128)(4,1)S(1)} %convert_compare_fusion.5), kind=kLoop, calls=%fused_computation.24.clone.1 | loop fusion | flops 25165824 | bytes 41961472 | tf_op jit(solution)/shard_map/while/body/eval_jaxpr/while/body/eval_jaxpr/convert_element_type | solution.py:88
  490.6 17.5 %scatter_custom_fusion = f32[12800,256]{1,0:T(8,128)} fusion(s32[2048]{0:T(1024)S(1)} %bitcast.187, f32[2048,256]{1,0:T(8,128)} %copy.90, f32[]{:T(128)} %constant.51.clone.1), kind=kCustom, calls=%fused_computation.57 | custom fusion | flops 524288 | bytes 13107712 | tf_op jit(solution)/shard_map/scatter-add | solution.py:281
  513.3 26.0 %reduce-scatter.15.cloned.1.call-done = f32[512,256]{0,1:T(8,128)} async-done(((f32[2048,256]{0,1:T(8,128)}), f32[512,256]{0,1:T(8,128)}) %reduce-scatter.15.cloned.1.call-update) | async-done | bytes 524304 | tf_op jit(solution)/shard_map/reduce_scatter | solution.py:307
  539.2 222.0 %reduce-scatter.9.cloned.1.call-done = f32[3200,256]{1,0:T(8,128)} async-done(((f32[12800,256]{1,0:T(8,128)}), f32[3200,256]{1,0:T(8,128)}) %reduce-scatter.9.cloned.1.call-update) | async-done | bytes 3276816 | tf_op jit(solution)/shard_map/reduce_scatter | solution.py:303
  761.3 11.3 %scatter_custom_fusion.1 = f32[12800]{0:T(1024)S(1)} fusion(s32[2048]{0:T(1024)S(1)} %bitcast.188, f32[2048]{0:T(1024)S(1)} %copy-done.36, f32[]{:T(128)} %constant.51.clone.1), kind=kCustom, calls=%fused_computation.126 | custom fusion | flops 2048 | bytes 51204 | tf_op jit(solution)/shard_map/scatter-add | solution.py:282
  780.6 19.4 %all-reduce.20 = (f32[12800]{0:T(1024)S(1)}, f32[256]{0:T(256)S(1)}, f32[256]{0:T(256)S(1)}, f32[256]{0:T(256)S(1)}, f32[256]{0:T(256)S(1)}, /*index=5*/f32[256]...) all-reduce(f32[12800]{0:T(1024)S(1)} %scatter_custom_fusion.1, ...), channel_id=3, replica_groups=mesh['dp'=8,'fsdp'=4] {'fsdp'}, use_global_device_ids=true, to_apply=%region_19.20.clone | all-reduce | flops 15360 | bytes 122880
  804.2 25.4 %all-reduce.18 = (f32[3200]{0:T(1024)S(1)}, f32[16,256]{1,0:T(8,128)}, f32[16,256]{1,0:T(8,128)}, f32[64]{0:T(128)}, f32[64]{0:T(128)}, /*index=5*/f32[64]{0:T(1...) all-reduce(f32[3200]{0:T(1024)S(1)} %dynamic-slice.14, ...), channel_id=1, replica_groups=mesh['dp'=8,'fsdp'=4] {'dp'}, use_global_device_ids=true, to_apply=%region_20.21 | all-reduce | flops 12032 | bytes 96256 | tf_op jit(solution)/shard_map/psum | solution.py:341
  830.2 60.0 %all-reduce.24.cloned.1.call-done = (f32[3200,256]{1,0:T(8,128)}, f32[512,256]{0,1:T(8,128)}, f32[64,768]{1,0:T(8,128)}, f32[64,256]{1,0:T(8,128)}, f32[64,512]{1,0:T(8,128)}, /*index=5*/f32[128,256]{1,0:T(8,128)}) async-done(((f32[3200,256]{1,0:T(8,128)}, f32[512,256]{0,1:T(8,128)}, f32[64,768]{1,0:T(8,128)}, f32[64,256]{1,0:T(8,128)}, f32[64,512]{1,0:T(8,128)}, /*index=5*/f32[128,256]{1,0:T(8,128)}), ...) | async-done | bytes 4325392 | tf_op jit(solution)/shard_map/psum | solution.py:341
  (340 shorter events, 296.4 us)
Async XLA Ops:
  7.2 160.6 %all-gather.4.cloned.1.call-start = ((), (), s32[]{:S(2)}) async-start(), calls=%async_computation.8 | async-start | bytes 8192000 | tf_op jit(solution)/shard_map/all_gather | solution.py:156
  7.9 173.8 %all-gather.6.cloned.1.call-start = ((), (), s32[]{:S(2)}) async-start(), calls=%async_computation.9 | async-start | bytes 1310720 | tf_op jit(solution)/shard_map/all_gather | solution.py:159
  9.8 503.4 %reduce-scatter.19.cloned.1.call-start = ((), (), s32[]{:S(2)}) async-start(), calls=%async_computation.15 | async-start | bytes 327680 | tf_op jit(solution)/shard_map/reduce_scatter | solution.py:313
  72.7 19.5 %copy-start.49 = (bf16[64,256]{1,0:T(8,128)(2,1)S(1)}, bf16[64,256]{1,0:T(8,128)(2,1)}, u32[]{:S(2)}) copy-start(bf16[64,256]{1,0:T(8,128)(2,1)} %param.42) | copy-start | bytes 98308
  72.7 38.4 %copy-start.44 = (bf16[64,512]{1,0:T(8,128)(2,1)S(1)}, bf16[64,512]{1,0:T(8,128)(2,1)}, u32[]{:S(2)}) copy-start(bf16[64,512]{1,0:T(8,128)(2,1)} %param.46) | copy-start | bytes 196612
  72.7 60.5 %copy-start.45 = (bf16[128,256]{1,0:T(8,128)(2,1)S(1)}, bf16[128,256]{1,0:T(8,128)(2,1)}, u32[]{:S(2)}) copy-start(bf16[128,256]{1,0:T(8,128)(2,1)} %param.48) | copy-start | bytes 196612
  73.4 94.4 %copy-start.50 = (s32[1,2048]{1,0:T(1,128)S(1)}, s32[1,2048]{1,0:T(1,128)}, u32[]{:S(2)}) copy-start(s32[1,2048]{1,0:T(1,128)} %param.27) | copy-start | bytes 24580
  150.7 31.0 %copy-start.34 = (f32[2048]{0:T(1024)}, f32[2048]{0:T(1024)S(1)}, u32[]{:S(2)}) copy-start(f32[2048]{0:T(1024)S(1)} %fusion.78) | copy-start | bytes 24580
  167.8 16.4 %copy-start.20 = (bf16[256,768]{1,0:T(8,128)(2,1)}, bf16[256,768]{1,0:T(8,128)(2,1)S(1)}, u32[]{:S(2)}) copy-start(bf16[256,768]{1,0:T(8,128)(2,1)S(1)} %all_gather.63) | copy-start | bytes 1179652
  167.8 13.9 %copy-start.63 = (f32[1,256]{1,0:T(1,128)S(1)}, f32[1,256]{1,0:T(1,128)}, u32[]{:S(2)}) copy-start(f32[1,256]{1,0:T(1,128)} %dynamic-slice_convert_fusion) | copy-start | bytes 3076
  248.9 11.5 %copy-start.4 = (f32[2048,256]{0,1:T(8,128)}, f32[2048,256]{0,1:T(8,128)S(1)}, u32[]{:S(2)}) copy-start(f32[2048,256]{0,1:T(8,128)S(1)} %get-tuple-element.435) | copy-start | bytes 6291460
  249.5 11.0 %copy-start.15 = (bf16[1,2048,256]{1,2,0:T(8,128)(2,1)S(1)}, bf16[1,2048,256]{1,2,0:T(8,128)(2,1)}, u32[]{:S(2)}) copy-start(bf16[1,2048,256]{1,2,0:T(8,128)(2,1)} %copy.83) | copy-start | bytes 3145732
  249.5 11.0 %copy-start.24 = (bf16[512,256]{1,0:T(8,128)(2,1)S(1)}, bf16[512,256]{1,0:T(8,128)(2,1)}, u32[]{:S(2)}) copy-start(bf16[512,256]{1,0:T(8,128)(2,1)} %all_gather.72) | copy-start | bytes 786436
  278.0 235.2 %reduce-scatter.21.cloned.1.call-start = ((), (), s32[]{:S(2)}) async-start(), calls=%async_computation.16 | async-start | bytes 655360 | tf_op jit(solution)/shard_map/reduce_scatter | solution.py:317
  281.9 231.4 %reduce-scatter.23.cloned.1.call-start = ((), (), s32[]{:S(2)}) async-start(), calls=%async_computation.17 | async-start | bytes 655360 | tf_op jit(solution)/shard_map/reduce_scatter | solution.py:319
  296.9 216.3 %reduce-scatter.17.cloned.1.call-start = ((), (), s32[]{:S(2)}) async-start(), calls=%async_computation.14 | async-start | bytes 983040 | tf_op jit(solution)/shard_map/reduce_scatter | solution.py:310
  472.8 66.5 %reduce-scatter.15.cloned.1.call-start = ((), (), s32[]{:S(2)}) async-start(), calls=%async_computation.13 | async-start | bytes 2621440 | tf_op jit(solution)/shard_map/reduce_scatter | solution.py:307
  487.2 274.0 %reduce-scatter.9.cloned.1.call-start = ((), (), s32[]{:S(2)}) async-start(), calls=%async_computation.10 | async-start | bytes 16384000 | tf_op jit(solution)/shard_map/reduce_scatter | solution.py:303
  508.1 292.7 %reduce-scatter.13.cloned.1.call-start = ((), (), s32[]{:S(2)}) async-start(), calls=%async_computation.12 | async-start | bytes 81920 | tf_op jit(solution)/shard_map/reduce_scatter | solution.py:306
  508.9 295.2 %reduce-scatter.11.cloned.1.call-start = ((), (), s32[]{:S(2)}) async-start(), calls=%async_computation.11 | async-start | bytes 81920 | tf_op jit(solution)/shard_map/reduce_scatter | solution.py:305
  509.2 265.3 %copy-start.71 = (bf16[256]{0:T(256)(128)(2,1)S(1)}, bf16[256]{0:T(256)(128)(2,1)}, u32[]{:S(2)}) copy-start(bf16[256]{0:T(256)(128)(2,1)} %get-tuple-element.412) | copy-start | bytes 1540
  509.2 265.3 %copy-start.6 = (f32[2048,256]{0,1:T(8,128)S(1)}, f32[2048,256]{0,1:T(8,128)}, u32[]{:S(2)}) copy-start(f32[2048,256]{0,1:T(8,128)} %copy-done.4) | copy-start | bytes 6291460
  509.2 265.3 %copy-start.25 = (bf16[512,256]{1,0:T(8,128)(2,1)S(1)}, bf16[512,256]{1,0:T(8,128)(2,1)}, u32[]{:S(2)}) copy-start(bf16[512,256]{1,0:T(8,128)(2,1)} %all_gather.72) | copy-start | bytes 786436
  513.1 377.1 %all-reduce.24.cloned.1.call-start = ((), (), s32[]{:S(2)}) async-start(), calls=%async_computation.18 | async-start | bytes 8650752 | tf_op jit(solution)/shard_map/psum | solution.py:341
  (63 other events, 219.0 us)
Sparse Core Ops, SparseCore 0:
  9.6 133.5 all-gather.3
  145.3 29.6 all-gather.5
  278.1 16.6 reduce-scatter.18
  297.6 19.8 reduce-scatter.20
  319.8 19.8 reduce-scatter.22
  472.9 20.1 reduce-scatter.16
  496.1 43.1 reduce-scatter.14
  541.6 219.6 reduce-scatter.8
  764.1 20.0 reduce-scatter.12
  786.9 17.1 reduce-scatter.10
  808.0 82.1 all-reduce.23
where the time goes:
time: 911 us; the launch traced here: 906 us
  waiting for transfers between devices  312 us (34%)
  matrix products  201 us (22%)
  blocking collectives  176 us (19%)
  other arithmetic  119 us (13%)
  local copies, waits for them, and re-layouts  77.5 us (9%)
  between operations  19.1 us (2%)
    reduce_scatter x1, waiting for transfers between devices, body(): lax.psum_scatter(dense_grad, 'fsdp', scatter_dimension=0, tiled=True)  222 us
    psum x1, waiting for transfers between devices, body(): lax.psum((table_share, count_share, expr_share, study_share, position_sha...  60 us
    convert_element_type x4, other arithmetic, one_block(): grad_scores = (probs * (grad_probs - inner)).astype(jnp.bfloat16)  42.7 us
    dot_general x4, matrix products, one_block(): jnp.einsum('qhk,shk->hqs', grad_block, values, preferred_element_type=jnp...  38.1 us
    unnamed x185, local copies, waits for them, and re-layouts  37.2 us
    unnamed x2, blocking collectives  35.6 us
    dot_general x4, matrix products, one_block(): jnp.einsum('hqs,shk->qhk', grad_scores, keys, preferred_element_type=jnp....  27.6 us
    dot_general x8, matrix products, one_block(): jnp.einsum('qhk,shk->hqs', query_block, keys, preferred_element_type=jnp....  27.3 us
  transfers between devices with their start and end apart: 11, of which 4 were waited for; matrix products, arithmetic and copies ran while one was open for 32% of the time, Pallas kernels for 0%

commit v1 on v0

--- a/solution.py
+++ b/solution.py
@@ -6,6 +6,14 @@
 HEADS = 4
 epsilon = 1e-05
 highest = lax.Precision.HIGHEST
+
+
+def gather_by_exchange(value, axis, dim):
+    peers = lax.axis_size(axis)
+    repeats = [peers if d == dim else 1 for d in range(value.ndim)]
+    return lax.all_to_all(
+        jnp.tile(value, repeats), axis, split_axis=dim, concat_axis=dim, tiled=True
+    )
 
 
 def normalize(values):
@@ -162,7 +170,7 @@
         lax.all_gather(w_qkv, "fsdp", axis=0, tiled=True),
         lax.all_gather(bias_query, "fsdp", axis=0, tiled=True),
         lax.all_gather(bias_value, "fsdp", axis=0, tiled=True),
-        lax.all_gather(w_output, "fsdp", axis=0, tiled=True),
+        gather_by_exchange(w_output, "fsdp", 0),
         lax.all_gather(bias_output, "fsdp", axis=0, tiled=True),
         lax.all_gather(norm2_gain, "fsdp", axis=0, tiled=True),
         lax.all_gather(norm2_shift, "fsdp", axis=0, tiled=True),

time: 911 us -> 920 us (level)
    unnamed x185 -> x179, local copies, waits for them, and re-layouts: 37.2 us -> 38.8 us
  transfers between devices with their start and end apart: 11 -> 12, of which waited for: 4 -> 5; matrix products, arithmetic and copies ran while one was open for 32% -> 39% of each run, Pallas kernels for 0% -> 0%
where the time goes in v1:
time: 920 us; the launch traced here: 915 us
  waiting for transfers between devices  320 us (35%)
  matrix products  202 us (22%)
  blocking collectives  167 us (18%)
  other arithmetic  119 us (13%)
  local copies, waits for them, and re-layouts  80.5 us (9%)
  between operations  19 us (2%)
    reduce_scatter x1, waiting for transfers between devices, body(): lax.psum_scatter(dense_grad, 'fsdp', scatter_dimension=0, tiled=True)  222 us
    psum x1, waiting for transfers between devices, body(): lax.psum((table_share, count_share, expr_share, study_share, position_sha...  60.2 us
    convert_element_type x4, other arithmetic, one_block(): grad_scores = (probs * (grad_probs - inner)).astype(jnp.bfloat16)  42.6 us
    unnamed x179, local copies, waits for them, and re-layouts  38.8 us
    dot_general x4, matrix products, one_block(): jnp.einsum('qhk,shk->hqs', grad_block, values, preferred_element_type=jnp...  37.6 us
    unnamed x2, blocking collectives  32.4 us
    reduce_scatter x1, waiting for transfers between devices, body(): lax.psum_scatter(grad_position, 'fsdp', scatter_dimension=0, tiled=True)  28.3 us
    dot_general x4, matrix products, one_block(): jnp.einsum('hqs,shk->qhk', grad_scores, keys, preferred_element_type=jnp....  27.6 us
  transfers between devices with their start and end apart: 12, of which 5 were waited for; matrix products, arithmetic and copies ran while one was open for 39% of the time, Pallas kernels for 0%

profile of v1, /device:TPU:0, one launch (start us, length us, event | category | flops | bytes accessed | tf_op | source)
XLA Modules:
  0.0 914.7 jit_solution(17489912226179058836)
XLA Ops:
  28.4 13.0 %all-reduce.21 = (bf16[256]{0:T(256)(128)(2,1)S(1)}, bf16[256]{0:T(256)(128)(2,1)S(1)}, bf16[256]{0:T(256)(128)(2,1)S(1)}, bf16[256]{0:T(256)(128)(2,1)S(1)}, bf...) all-reduce(bf16[256]{0:T(256)(128)(2,1)S(1)} %dynamic-update-slice., ...), channel_id=1, replica_groups=mesh['dp'=8,'fsdp'=4] {'fsdp'}, use_global_device_ids=true, to_apply=%add.1 | all-reduce | flops 2048 | bytes 8192
  45.2 11.1 %all-gather = bf16[4,1,128]{2,1,0:T(2,128)(2,1)S(1)} all-gather(bf16[1,1,128]{2,1,0:T(2,128)(2,1)} %bitcast.193), channel_id=1, replica_groups=mesh['dp'=8,'fsdp'=4] {'fsdp'}, dimensions={0}, use_global_device_ids=true | all-gather | bytes 1280 | tf_op jit(solution)/shard_map/all_gather | solution.py:178
  56.9 15.9 %all_gather.57 = bf16[64,256]{1,0:T(8,128)(2,1)S(1)} all-gather(bf16[16,256]{1,0:T(8,128)(2,1)} %param.34), channel_id=1, replica_groups=mesh['dp'=8,'fsdp'=4] {'fsdp'}, dimensions={0}, use_global_device_ids=true | all-gather | bytes 40960 | tf_op jit(solution)/shard_map/all_gather | solution.py:165
  83.9 15.9 %all_gather.58 = bf16[64,256]{1,0:T(8,128)(2,1)S(1)} all-gather(bf16[16,256]{1,0:T(8,128)(2,1)S(1)} %copy-done.52), channel_id=1, replica_groups=mesh['dp'=8,'fsdp'=4] {'fsdp'}, dimensions={0}, use_global_device_ids=true | all-gather | bytes 40960 | tf_op jit(solution)/shard_map/all_gather | solution.py:166
  99.8 20.6 %all_gather.68 = bf16[256,512]{1,0:T(8,128)(2,1)} all-gather(bf16[64,512]{1,0:T(8,128)(2,1)S(1)} %copy-done.42), channel_id=1, replica_groups=mesh['dp'=8,'fsdp'=4] {'fsdp'}, dimensions={0}, use_global_device_ids=true | all-gather | bytes 327680 | tf_op jit(solution)/shard_map/all_gather | solution.py:177
  120.4 16.7 %all_gather.70 = bf16[512,256]{1,0:T(8,128)(2,1)} all-gather(bf16[128,256]{1,0:T(8,128)(2,1)S(1)} %copy-done.43), channel_id=1, replica_groups=mesh['dp'=8,'fsdp'=4] {'fsdp'}, dimensions={0}, use_global_device_ids=true | all-gather | bytes 327680 | tf_op jit(solution)/shard_map/all_gather | solution.py:179
  137.7 15.0 %all_gather.62 = bf16[256,768]{1,0:T(8,128)(2,1)S(1)} all-gather(bf16[64,768]{1,0:T(8,128)(2,1)} %param.39), channel_id=1, replica_groups=mesh['dp'=8,'fsdp'=4] {'fsdp'}, dimensions={0}, use_global_device_ids=true | all-gather | bytes 491520 | tf_op jit(solution)/shard_map/all_gather | solution.py:170
  152.8 12.3 %gather_fusion = bf16[2048,256]{1,0:T(8,128)(2,1)} fusion(bf16[12800,256]{1,0:T(8,128)(2,1)} %all-gather.4.cloned.1.call-done, s32[2048]{0:T(1024)S(1)} %broadcast_clamp_fusion.1), kind=kCustom, calls=%fused_computation | custom fusion | bytes 2105344 | tf_op jit(solution)/shard_map/gather | solution.py:197
  183.0 53.9 %while.49 = (s32[]{:T(128)}, bf16[4,512,4,64]{1,3,2,0:T(8,128)(2,1)}, f32[4,4,512]{2,1,0:T(4,128)S(1)}, bf16[4,512,4,64]{1,3,2,0:T(8,128)(2,1)}, bf16[2048,4,64]...) while((s32[]{:T(128)}, bf16[4,512,4,64]{1,3,2,0:T(8,128)(2,1)}, ...), condition=%wide.region_5.6_spmd.clone, body=%wide.region_2.5_spmd.clone.sunk | while | flops 1124208640 | bytes 53026924 | solution.py:72
  243.1 10.9 %multiply_convert_fusion.1 = (bf16[2048,512]{1,0:T(8,128)(2,1)}, f32[2048,512]{1,0:T(8,128)S(1)}, f32[2048,512]{1,0:T(8,128)S(1)}) fusion(f32[512]{0:T(512)S(1)} %bitcast.191, bf16[256,512]{1,0:T(8,128)(2,1)S(1)} %copy-done.23, f32[2048,256]{0,1:T(8,128)S(1)} %get-tuple-element.435, f32[256]{0:T(256)S(1)} %copy-done.69, f32[256]{0:T(256)S(1)} %copy-done.61, ...), kind=kOutput, calls=%fused_computation.63 | convolution fusion | flops 608698368 | bytes 12865536 | tf_op jit(solution)/shard_map/dot_general | solution.py:33
  275.5 14.0 %all_gather.72 = bf16[256,256]{1,0:T(8,128)(2,1)S(1)} all-gather(bf16[64,256]{1,0:T(8,128)(2,1)S(1)} %copy-done.35), channel_id=1, replica_groups=mesh['dp'=8,'fsdp'=4] {'fsdp'}, dimensions={0}, use_global_device_ids=true | all-gather | bytes 163840 | tf_op jit(solution)/shard_map/all_gather | solution.py:230
  304.4 166.1 %while.50 = (s32[]{:T(128)}, f32[2048,4,64]{0,2,1:T(8,128)}, f32[2048,4,64]{0,2,1:T(8,128)}, bf16[4,512,4,64]{1,3,2,0:T(8,128)(2,1)}, bf16[4,512,4,64]{1,3,2,0:T...) while((s32[]{:T(128)}, f32[2048,4,64]{0,2,1:T(8,128)}, ...), condition=%wide.region_12.13_spmd.clone, body=%wide.region_10.12_spmd.clone.sunk | while | flops 2750025728 | bytes 172556464 | solution.py:114
  314.2 9.4 %multiply_reduce_fusion.8 = (f32[4,512]{1,0:T(4,128)S(1)}, f32[4,512,2048]{2,1,0:T(8,128)}) fusion(f32[4,512,2048]{2,1,0:T(8,128)S(1)} %fusion.154, f32[4,512]{1,0:T(4,128)S(1)} %dynamic-slice_bitcast_fusion.2, pred[2048]{0:T(1024)(128)(4,1)S(1)} %convert_compare_fusion.5, bf16[2048,4,64]{0,2,1:T(8,128)(2,1)S(1)} %get-tuple-element.611, ...), kind=kOutput, calls=%fused_computation.25.clone.1 | convolution fusion | flops 557840384 | bytes 34883588 | tf_op jit(solution)/shard_map/while/body/eval_jaxpr/while/body/eval_jaxpr/qhk,shk->hqs/dot_general | solution.py:92
  323.6 10.7 %multiply_convert_fusion.3 = bf16[4,512,2048]{2,1,0:T(8,128)(2,1)} fusion(f32[4,512,2048]{2,1,0:T(8,128)} %get-tuple-element.553, f32[4,512,2048]{2,1,0:T(8,128)S(1)} %fusion.154, f32[4,512]{1,0:T(4,128)S(1)} %get-tuple-element.554, f32[4,512]{1,0:T(4,128)S(1)} %dynamic-slice_bitcast_fusion.2, pred[2048]{0:T(1024)(128)(4,1)S(1)} %convert_compare_fusion.5), kind=kLoop, calls=%fused_computation.24.clone.1 | loop fusion | flops 25165824 | bytes 41961472 | tf_op jit(solution)/shard_map/while/body/eval_jaxpr/while/body/eval_jaxpr/convert_element_type | solution.py:96
  364.7 10.6 %multiply_convert_fusion.3 = bf16[4,512,2048]{2,1,0:T(8,128)(2,1)} fusion(f32[4,512,2048]{2,1,0:T(8,128)} %get-tuple-element.553, f32[4,512,2048]{2,1,0:T(8,128)S(1)} %fusion.154, f32[4,512]{1,0:T(4,128)S(1)} %get-tuple-element.554, f32[4,512]{1,0:T(4,128)S(1)} %dynamic-slice_bitcast_fusion.2, pred[2048]{0:T(1024)(128)(4,1)S(1)} %convert_compare_fusion.5), kind=kLoop, calls=%fused_computation.24.clone.1 | loop fusion | flops 25165824 | bytes 41961472 | tf_op jit(solution)/shard_map/while/body/eval_jaxpr/while/body/eval_jaxpr/convert_element_type | solution.py:96
  406.5 10.6 %multiply_convert_fusion.3 = bf16[4,512,2048]{2,1,0:T(8,128)(2,1)} fusion(f32[4,512,2048]{2,1,0:T(8,128)} %get-tuple-element.553, f32[4,512,2048]{2,1,0:T(8,128)S(1)} %fusion.154, f32[4,512]{1,0:T(4,128)S(1)} %get-tuple-element.554, f32[4,512]{1,0:T(4,128)S(1)} %dynamic-slice_bitcast_fusion.2, pred[2048]{0:T(1024)(128)(4,1)S(1)} %convert_compare_fusion.5), kind=kLoop, calls=%fused_computation.24.clone.1 | loop fusion | flops 25165824 | bytes 41961472 | tf_op jit(solution)/shard_map/while/body/eval_jaxpr/while/body/eval_jaxpr/convert_element_type | solution.py:96
  448.2 10.6 %multiply_convert_fusion.3 = bf16[4,512,2048]{2,1,0:T(8,128)(2,1)} fusion(f32[4,512,2048]{2,1,0:T(8,128)} %get-tuple-element.553, f32[4,512,2048]{2,1,0:T(8,128)S(1)} %fusion.154, f32[4,512]{1,0:T(4,128)S(1)} %get-tuple-element.554, f32[4,512]{1,0:T(4,128)S(1)} %dynamic-slice_bitcast_fusion.2, pred[2048]{0:T(1024)(128)(4,1)S(1)} %convert_compare_fusion.5), kind=kLoop, calls=%fused_computation.24.clone.1 | loop fusion | flops 25165824 | bytes 41961472 | tf_op jit(solution)/shard_map/while/body/eval_jaxpr/while/body/eval_jaxpr/convert_element_type | solution.py:96
  497.3 17.5 %scatter_custom_fusion = f32[12800,256]{1,0:T(8,128)} fusion(s32[2048]{0:T(1024)S(1)} %bitcast.188, f32[2048,256]{1,0:T(8,128)} %copy.90, f32[]{:T(128)} %constant.51.clone.1), kind=kCustom, calls=%fused_computation.57 | custom fusion | flops 524288 | bytes 13107712 | tf_op jit(solution)/shard_map/scatter-add | solution.py:289
  520.0 28.3 %reduce-scatter.15.cloned.1.call-done = f32[512,256]{0,1:T(8,128)} async-done(((f32[2048,256]{0,1:T(8,128)}), f32[512,256]{0,1:T(8,128)}) %reduce-scatter.15.cloned.1.call-update) | async-done | bytes 524304 | tf_op jit(solution)/shard_map/reduce_scatter | solution.py:315
  548.3 222.0 %reduce-scatter.9.cloned.1.call-done = f32[3200,256]{1,0:T(8,128)} async-done(((f32[12800,256]{1,0:T(8,128)}), f32[3200,256]{1,0:T(8,128)}) %reduce-scatter.9.cloned.1.call-update) | async-done | bytes 3276816 | tf_op jit(solution)/shard_map/reduce_scatter | solution.py:311
  770.3 11.3 %scatter_custom_fusion.1 = f32[12800]{0:T(1024)S(1)} fusion(s32[2048]{0:T(1024)S(1)} %bitcast.189, f32[2048]{0:T(1024)S(1)} %copy-done.33, f32[]{:T(128)} %constant.51.clone.1), kind=kCustom, calls=%fused_computation.126 | custom fusion | flops 2048 | bytes 51204 | tf_op jit(solution)/shard_map/scatter-add | solution.py:290
  789.7 19.5 %all-reduce.20 = (f32[12800]{0:T(1024)S(1)}, f32[256]{0:T(256)S(1)}, f32[256]{0:T(256)S(1)}, f32[256]{0:T(256)S(1)}, f32[256]{0:T(256)S(1)}, /*index=5*/f32[256]...) all-reduce(f32[12800]{0:T(1024)S(1)} %scatter_custom_fusion.1, ...), channel_id=3, replica_groups=mesh['dp'=8,'fsdp'=4] {'fsdp'}, use_global_device_ids=true, to_apply=%region_19.20.clone | all-reduce | flops 15360 | bytes 122880
  813.2 25.4 %all-reduce.18 = (f32[3200]{0:T(1024)S(1)}, f32[16,256]{1,0:T(8,128)}, f32[16,256]{1,0:T(8,128)}, f32[64]{0:T(128)}, f32[64]{0:T(128)}, /*index=5*/f32[64]{0:T(1...) all-reduce(f32[3200]{0:T(1024)S(1)} %dynamic-slice.14, ...), channel_id=1, replica_groups=mesh['dp'=8,'fsdp'=4] {'dp'}, use_global_device_ids=true, to_apply=%region_20.21 | all-reduce | flops 12032 | bytes 96256 | tf_op jit(solution)/shard_map/psum | solution.py:349
  839.2 60.2 %all-reduce.24.cloned.1.call-done = (f32[3200,256]{1,0:T(8,128)}, f32[512,256]{0,1:T(8,128)}, f32[64,768]{1,0:T(8,128)}, f32[64,256]{1,0:T(8,128)}, f32[64,512]{1,0:T(8,128)}, /*index=5*/f32[128,256]{1,0:T(8,128)}) async-done(((f32[3200,256]{1,0:T(8,128)}, f32[512,256]{0,1:T(8,128)}, f32[64,768]{1,0:T(8,128)}, f32[64,256]{1,0:T(8,128)}, f32[64,512]{1,0:T(8,128)}, /*index=5*/f32[128,256]{1,0:T(8,128)}), ...) | async-done | bytes 4325392 | tf_op jit(solution)/shard_map/psum | solution.py:349
  (337 shorter events, 313.9 us)
Async XLA Ops:
  7.2 145.6 %all-gather.4.cloned.1.call-start = ((), (), s32[]{:S(2)}) async-start(), calls=%async_computation.9 | async-start | bytes 8192000 | tf_op jit(solution)/shard_map/all_gather | solution.py:164
  9.3 230.8 %all-to-all-start = ((bf16[4,64,256]{2,1,0:T(8,128)(2,1)}), bf16[4,64,256]{2,1,0:T(8,128)(2,1)}, u32[]{:S(2)}, u32[]{:S(2)}) async-start(bf16[4,64,256]{2,1,0:T(8,128)(2,1)} %tile.2), calls=%async_computation | async-start | bytes 262144 | tf_op jit(solution)/shard_map/all_to_all | solution.py:14
  15.7 156.2 %all-gather.6.cloned.1.call-start = ((), (), s32[]{:S(2)}) async-start(), calls=%async_computation.10 | async-start | bytes 1310720 | tf_op jit(solution)/shard_map/all_gather | solution.py:167
  17.5 502.4 %reduce-scatter.19.cloned.1.call-start = ((), (), s32[]{:S(2)}) async-start(), calls=%async_computation.16 | async-start | bytes 327680 | tf_op jit(solution)/shard_map/reduce_scatter | solution.py:321
  80.3 19.6 %copy-start.42 = (bf16[64,512]{1,0:T(8,128)(2,1)S(1)}, bf16[64,512]{1,0:T(8,128)(2,1)}, u32[]{:S(2)}) copy-start(bf16[64,512]{1,0:T(8,128)(2,1)} %param.46) | copy-start | bytes 196612
  80.3 40.1 %copy-start.43 = (bf16[128,256]{1,0:T(8,128)(2,1)S(1)}, bf16[128,256]{1,0:T(8,128)(2,1)}, u32[]{:S(2)}) copy-start(bf16[128,256]{1,0:T(8,128)(2,1)} %param.48) | copy-start | bytes 196612
  81.0 71.7 %copy-start.47 = (s32[1,2048]{1,0:T(1,128)S(1)}, s32[1,2048]{1,0:T(1,128)}, u32[]{:S(2)}) copy-start(s32[1,2048]{1,0:T(1,128)} %param.27) | copy-start | bytes 24580
  137.7 34.1 %copy-start.31 = (f32[2048]{0:T(1024)}, f32[2048]{0:T(1024)S(1)}, u32[]{:S(2)}) copy-start(f32[2048]{0:T(1024)S(1)} %fusion.78) | copy-start | bytes 24580
  152.7 21.6 %copy-start.18 = (bf16[256,768]{1,0:T(8,128)(2,1)}, bf16[256,768]{1,0:T(8,128)(2,1)S(1)}, u32[]{:S(2)}) copy-start(bf16[256,768]{1,0:T(8,128)(2,1)S(1)} %all_gather.62) | copy-start | bytes 1179652
  152.7 19.1 %copy-start.60 = (f32[1,256]{1,0:T(1,128)S(1)}, f32[1,256]{1,0:T(1,128)}, u32[]{:S(2)}) copy-start(f32[1,256]{1,0:T(1,128)} %dynamic-slice_convert_fusion) | copy-start | bytes 3076
  242.7 11.3 %copy-start.3 = (f32[2048,256]{0,1:T(8,128)}, f32[2048,256]{0,1:T(8,128)S(1)}, u32[]{:S(2)}) copy-start(f32[2048,256]{0,1:T(8,128)S(1)} %get-tuple-element.435) | copy-start | bytes 6291460
  243.0 10.9 %copy-start.13 = (bf16[1,2048,256]{1,2,0:T(8,128)(2,1)S(1)}, bf16[1,2048,256]{1,2,0:T(8,128)(2,1)}, u32[]{:S(2)}) copy-start(bf16[1,2048,256]{1,2,0:T(8,128)(2,1)} %copy.83) | copy-start | bytes 3145732
  243.1 10.9 %copy-start.21 = (bf16[512,256]{1,0:T(8,128)(2,1)S(1)}, bf16[512,256]{1,0:T(8,128)(2,1)}, u32[]{:S(2)}) copy-start(bf16[512,256]{1,0:T(8,128)(2,1)} %all_gather.70) | copy-start | bytes 786436
  271.5 248.4 %reduce-scatter.21.cloned.1.call-start = ((), (), s32[]{:S(2)}) async-start(), calls=%async_computation.17 | async-start | bytes 655360 | tf_op jit(solution)/shard_map/reduce_scatter | solution.py:325
  275.4 244.6 %reduce-scatter.23.cloned.1.call-start = ((), (), s32[]{:S(2)}) async-start(), calls=%async_computation.18 | async-start | bytes 655360 | tf_op jit(solution)/shard_map/reduce_scatter | solution.py:327
  304.4 215.6 %reduce-scatter.17.cloned.1.call-start = ((), (), s32[]{:S(2)}) async-start(), calls=%async_computation.15 | async-start | bytes 983040 | tf_op jit(solution)/shard_map/reduce_scatter | solution.py:318
  479.5 68.8 %reduce-scatter.15.cloned.1.call-start = ((), (), s32[]{:S(2)}) async-start(), calls=%async_computation.14 | async-start | bytes 2621440 | tf_op jit(solution)/shard_map/reduce_scatter | solution.py:315
  493.9 276.4 %reduce-scatter.9.cloned.1.call-start = ((), (), s32[]{:S(2)}) async-start(), calls=%async_computation.11 | async-start | bytes 16384000 | tf_op jit(solution)/shard_map/reduce_scatter | solution.py:311
  514.8 295.0 %reduce-scatter.13.cloned.1.call-start = ((), (), s32[]{:S(2)}) async-start(), calls=%async_computation.13 | async-start | bytes 81920 | tf_op jit(solution)/shard_map/reduce_scatter | solution.py:314
  515.6 297.5 %reduce-scatter.11.cloned.1.call-start = ((), (), s32[]{:S(2)}) async-start(), calls=%async_computation.12 | async-start | bytes 81920 | tf_op jit(solution)/shard_map/reduce_scatter | solution.py:313
  515.9 267.6 %copy-start.68 = (bf16[256]{0:T(256)(128)(2,1)S(1)}, bf16[256]{0:T(256)(128)(2,1)}, u32[]{:S(2)}) copy-start(bf16[256]{0:T(256)(128)(2,1)} %get-tuple-element.412) | copy-start | bytes 1540
  515.9 267.6 %copy-start.5 = (f32[2048,256]{0,1:T(8,128)S(1)}, f32[2048,256]{0,1:T(8,128)}, u32[]{:S(2)}) copy-start(f32[2048,256]{0,1:T(8,128)} %copy-done.3) | copy-start | bytes 6291460
  515.9 267.6 %copy-start.22 = (bf16[512,256]{1,0:T(8,128)(2,1)S(1)}, bf16[512,256]{1,0:T(8,128)(2,1)}, u32[]{:S(2)}) copy-start(bf16[512,256]{1,0:T(8,128)(2,1)} %all_gather.70) | copy-start | bytes 786436
  519.8 379.5 %all-reduce.24.cloned.1.call-start = ((), (), s32[]{:S(2)}) async-start(), calls=%async_computation.19 | async-start | bytes 8650752 | tf_op jit(solution)/shard_map/psum | solution.py:349
  (61 other events, 227.9 us)
Sparse Core Ops, SparseCore 0:
  9.6 133.9 all-gather.3
  145.7 26.0 all-gather.5
  271.6 19.7 reduce-scatter.18
  294.2 19.8 reduce-scatter.20
  316.4 19.8 reduce-scatter.22
  479.6 22.4 reduce-scatter.16
  505.1 43.1 reduce-scatter.14
  550.7 219.5 reduce-scatter.8
  773.1 20.0 reduce-scatter.12
  795.9 17.1 reduce-scatter.10
  817.0 82.2 all-reduce.23
